TPU v7x, 256 devices: a whole 4x4x8 slice. The times are simulated.
256 devices in a mesh: rollout: 2 (over core), context: 32 (over z, x), head: 4 (over y).
Axes of the slice: x: 4, y: 4, z: 8, core: 2. Of those that a mesh axis runs over, the one named last changes fastest.
Arguments:
- inner_raw: bfloat16 [16384, 8192], P(('rollout', 'context', 'head')), parts along dimension 0, may hold values from -6 to 6
- pairs_raw: bfloat16 [16384, 8, 2, 128], P(('rollout', 'context', 'head')), parts along dimension 0, may hold values from -2.5 to 2.5
- gate_raw: bfloat16 [16384, 8192], P(('rollout', 'context'), 'head'), parts along dimension 0, may hold values from -6 to 6
- step_raw: bfloat16 [16384, 128], P(('rollout', 'context'), 'head'), parts along dimension 0, may hold values from -3 to 3
- step_bias: float32 [128], P('head'), may hold values from -0.5 to 0.5
- rate_log: float32 [128], P('head'), may hold values from -13.5 to -2.8, as said below
- skip_gain: float32 [128], P('head'), may hold values from 0.5 to 2
- conv_inner: float32 [5, 8192], replicated, may hold values from -2.5 to 2.5
- conv_pairs: float32 [5, 8, 2, 128], replicated, may hold values from -2.5 to 2.5
- norm_gain: float32 [8192], P('head'), may hold values from 0.5 to 1.5
Outputs:
- mixer_out: bfloat16 [16384, 8192], P(('rollout', 'context', 'head')), parts along dimension 0
There are 2 independent parts, one for each index of `rollout`. A program takes and returns all parts, laid end to end along the dimension named above; an argument that names none is the same for every part. Nothing has to cross between parts.
Inputs may be any that keep to these rules, and one draw needn't show every extreme that they name: `rate_log`: one value a head.
All inputs are finite; a program needn't handle non-finite values.
Results may differ from a plain program's by a relative error of at most 0.012.
The roundings to bfloat16 on the way count: a program that leaves them out, or rounds other values in their place, can miss the bound.
Values may be sent and summed in bfloat16 or wider, within the bound.
No kernel may reach another device: no remote copies, remote signals or barrier semaphores. Data moves between devices by JAX's collectives and lax.ppermute only.
A program may use at most 128 MiB of HBM per device.

v0:
```python
import jax
import jax.numpy as jnp
from jax import lax
from jax.sharding import PartitionSpec as P

BLOCK = 256


def from_behind(block, axis, distance):
    devices = range(lax.axis_size(axis))
    route = [(i - distance, i) for i in devices if i - distance in devices]
    return lax.ppermute(block, axis, route)


def prefix(part, axis, combine, identity):
    place = lax.axis_index(axis)
    gathered = jax.tree.map(lambda a: lax.all_gather(a, axis), part)
    state = jax.tree.map(lambda a, e: jnp.zeros_like(a) + jnp.asarray(e, a.dtype), part, identity)

    def one(lap, state):
        return combine(
            state, jax.tree.map(lambda a: lax.dynamic_index_in_dim(a, lap, 0, False), gathered)
        )

    return lax.fori_loop(0, place, one, state)


def convolve(raw_rows, before, weight):
    tap_count = weight.shape[0] - 1
    row_count = raw_rows.shape[0]
    extended = jnp.concatenate([before, raw_rows], axis=0).astype(jnp.float32)
    summed = weight[tap_count][None, :] + weight[0][None, :] * extended[0:row_count]
    for offset in range(1, tap_count):
        summed = summed + weight[offset][None, :] * extended[offset : offset + row_count]
    return jax.nn.silu(summed).astype(jnp.bfloat16)


def block_intra(inner_conv, pairs_conv, step_size, log_cum, groups):
    block_len, head_count = step_size.shape
    per_group = head_count // groups
    head_width = inner_conv.shape[1] // head_count
    pair_view = pairs_conv.reshape(block_len, groups, 2, -1)
    scores = jnp.einsum(
        "ign,jgn->gij", pair_view[:, :, 1], pair_view[:, :, 0], preferred_element_type=jnp.float32
    )
    lower_tri = lax.broadcasted_iota(jnp.int32, (block_len, block_len), 0) >= lax.broadcasted_iota(
        jnp.int32, (block_len, block_len), 1
    )
    cum_t = log_cum.T
    log_gap = jnp.minimum(cum_t[:, :, None] - cum_t[:, None, :], 0.0)
    decay_mat = jnp.where(lower_tri[None], jnp.exp(log_gap), 0.0) * step_size.T[:, None, :]
    weights = (scores[:, None] * decay_mat.reshape(groups, per_group, block_len, block_len)).astype(
        jnp.bfloat16
    )
    inner_view = inner_conv.reshape(block_len, groups, per_group, head_width)
    intra_out = jnp.einsum(
        "gkij,jgkp->igkp", weights, inner_view, preferred_element_type=jnp.float32
    )
    return intra_out.reshape(block_len, head_count * head_width)


def block_state(inner_conv, pairs_conv, step_size, log_cum, groups):
    block_len, head_count = step_size.shape
    per_group = head_count // groups
    head_width = inner_conv.shape[1] // head_count
    tail_w = jnp.exp(log_cum[-1][None, :] - log_cum) * step_size
    weighted = (
        inner_conv.reshape(block_len, head_count, head_width).astype(jnp.float32)
        * tail_w[:, :, None]
    ).astype(jnp.bfloat16)
    weighted = weighted.reshape(block_len, groups, per_group, head_width)
    bmat = pairs_conv.reshape(block_len, groups, 2, -1)[:, :, 0]
    local_state = jnp.einsum("jgn,jgkp->gknp", bmat, weighted, preferred_element_type=jnp.float32)
    return (local_state.reshape(head_count, -1, head_width), jnp.exp(log_cum[-1]))


def finish(
    inner_conv, pairs_conv, gate_rows, intra_out, carry_state, log_cum, skip_gain, norm_gain, groups
):
    block_len, head_count = log_cum.shape
    per_group = head_count // groups
    head_width = inner_conv.shape[1] // head_count
    cmat = pairs_conv.reshape(block_len, groups, 2, -1)[:, :, 1]
    held = carry_state.astype(jnp.bfloat16).reshape(groups, per_group, -1, head_width)
    carried = jnp.einsum("ign,gknp->igkp", cmat, held, preferred_element_type=jnp.float32)
    carried = carried.reshape(block_len, head_count, head_width) * jnp.exp(log_cum)[:, :, None]
    mixed = (
        intra_out
        + carried.reshape(block_len, -1)
        + jnp.repeat(skip_gain, head_width)[None, :] * inner_conv.astype(jnp.float32)
    )
    gated_out = mixed * jax.nn.silu(gate_rows.astype(jnp.float32))
    grouped = gated_out.reshape(block_len, groups, -1)
    inv_rms = lax.rsqrt(jnp.mean(grouped * grouped, axis=2, keepdims=True) + 1e-05)
    return ((grouped * inv_rms).reshape(block_len, -1) * norm_gain[None, :]).astype(jnp.bfloat16)


def chain_combine(earlier, later):
    return (earlier[0] * later[0], later[0][:, None, None] * earlier[1] + later[1])


def absorb(running, element):
    local_state, block_decay = element
    return (block_decay[:, None, None] * running + local_state, None)


def on_device(
    inner_raw,
    pairs_raw,
    gate_raw,
    step_raw,
    step_bias,
    rate_log,
    skip_gain,
    conv_inner,
    conv_pairs,
    norm_gain,
):
    shards = lax.axis_size("head")
    row_count = inner_raw.shape[0]
    tap_count = conv_inner.shape[0] - 1
    inner_full = inner_raw.shape[1]
    pairs_flat = pairs_raw.reshape(row_count, -1)
    conv_flat = conv_pairs.reshape(tap_count + 1, -1)
    width_local = gate_raw.shape[1]
    head_local = step_raw.shape[1]
    groups_local = pairs_raw.shape[1] // shards
    last_rows = jnp.concatenate(
        [inner_raw[row_count - tap_count :], pairs_flat[row_count - tap_count :]], axis=1
    )
    before = from_behind(last_rows, ("context", "head"), 1)
    outgoing_inner = convolve(inner_raw, before[:, :inner_full], conv_inner)
    outgoing_pairs = convolve(pairs_flat, before[:, inner_full:], conv_flat)
    got_inner, got_pairs = (
        lax.all_to_all(outgoing_inner, "head", split_axis=1, concat_axis=0, tiled=True),
        lax.all_to_all(outgoing_pairs, "head", split_axis=1, concat_axis=0, tiled=True),
    )
    length = got_inner.shape[0]
    block_count = length // BLOCK
    step_size = jax.nn.softplus(step_raw.astype(jnp.float32) + step_bias[None, :])
    log_steps = (-jnp.exp(rate_log)[None, :] * step_size).reshape(block_count, BLOCK, head_local)
    lower_tri = (
        lax.broadcasted_iota(jnp.int32, (BLOCK, BLOCK), 0)
        >= lax.broadcasted_iota(jnp.int32, (BLOCK, BLOCK), 1)
    ).astype(jnp.float32)
    log_cum = jnp.einsum("ij,cjh->cih", lower_tri, log_steps, precision=lax.Precision.HIGHEST)
    step_blocks = step_size.reshape(block_count, BLOCK, head_local)
    inner_blocks = got_inner.reshape(block_count, BLOCK, -1)
    pair_blocks = got_pairs.reshape(block_count, BLOCK, -1)
    gate_blocks = gate_raw.reshape(block_count, BLOCK, -1)
    inputs = (inner_blocks, pair_blocks, step_blocks, log_cum)

    def intra_part(element):
        return block_intra(element[0], element[1], element[2], element[3], groups_local)

    def state_part(element):
        return block_state(element[0], element[1], element[2], element[3], groups_local)

    def both_parts(element):
        local_state, block_decay = state_part(element)
        return (intra_part(element), local_state, block_decay)

    intra_all, states, decays = lax.map(both_parts, inputs)
    start_zero = jnp.zeros(states.shape[1:], jnp.float32)
    device_state, _ = lax.scan(absorb, start_zero, (states, decays))
    device_decay = jnp.prod(decays, axis=0)
    incoming = prefix(
        (device_decay, device_state),
        "context",
        chain_combine,
        (jnp.ones_like(device_decay), jnp.zeros_like(device_state)),
    )

    def emit(carry_state, element):
        inner_rows, pair_rows, gate_rows, intra_out, cum_rows, local_state, block_decay = element
        result = finish(
            inner_rows,
            pair_rows,
            gate_rows,
            intra_out,
            carry_state,
            cum_rows,
            skip_gain,
            norm_gain,
            groups_local,
        )
        return (block_decay[:, None, None] * carry_state + local_state, result)

    _, results = lax.scan(
        emit,
        incoming[1],
        (inner_blocks, pair_blocks, gate_blocks, intra_all, log_cum, states, decays),
    )
    head_rows = results.reshape(length, width_local)
    return lax.all_to_all(head_rows, "head", split_axis=0, concat_axis=1, tiled=True)


def solution(mesh):
    placed = (
        P(("rollout", "context", "head"), None),
        P(("rollout", "context", "head"), None, None, None),
        P(("rollout", "context"), "head"),
        P(("rollout", "context"), "head"),
        P("head"),
        P("head"),
        P("head"),
        P(),
        P(),
        P("head"),
    )
    return jax.shard_map(
        on_device,
        mesh=mesh,
        in_specs=placed,
        out_specs=P(("rollout", "context", "head"), None),
        check_vma=False,
    )
```

profile of v0, /device:TPU:230, one launch (start us, length us, event | category | flops | bytes accessed | tf_op | source)
XLA Modules:
  0.0 496.4 jit_solution(1473578907943598542)
XLA Ops:
  8.3 3.5 collective-permute-start
  13.3 1.7 fusion.49
  19.2 4.2 all-to-all-start.1
  23.7 1.3 multiply_convert_fusion.2
  26.1 4.0 all-to-all-done.1
  30.0 3.5 all-to-all-start
  36.2 11.0 %all-to-all-done = bf16[64,4,2048]{2,0,1:T(8,128)(2,1)S(1)} async-done(((bf16[64,4,2048]{2,0,1:T(8,128)(2,1)}), bf16[64,4,2048]{2,0,1:T(8,128)(2,1)S(1)}, u32[]{:S(2)}, u32[]{:S(2)}) %all-to-all-start) | async-done | bytes 1048608 | tf_op jit(solution)/shard_map/all_to_all | solution.py:135
  47.2 2.2 reshape.197
  49.4 2.5 copy.90
  51.9 1.7 fusion.23
  58.4 38.2 %all-gather = f32[32,1,32]{2,1,0:T(1,128)} all-gather(f32[1,1,32]{2,1,0:T(1,128)S(1)} %get-tuple-element.157), channel_id=2, replica_groups=mesh['rollout'=2,'context'=32,'head'=4] {'context'}, dimensions={0}, use_global_device_ids=true | all-gather | bytes 4224 | tf_op jit(solution)/shard_map/all_gather | solution.py:17
  98.6 1.8 copy.97
  100.4 5.3 %fusion = f32[2,16,64,256]{3,2,1,0:T(8,128)} fusion(bf16[256,2,16,64]{0,3,2,1:T(8,128)(2,1)S(1)} %copy-done.1, f32[2,16,256]{2,1,0:T(8,128)S(1)} %bitcast.138, f32[2,16,256]{2,1,0:T(8,128)S(1)} %bitcast.136, f32[2,256,256]{2,1,0:T(8,128)} %fusion.35, pred[256,256]{1,0:T(8,128)(4,1)S(1)} %copy-done.11), kind=kOutput, calls=%fused_computation.4 | convolution fusion | flops 281018368 | bytes 3801088 | tf_op jit(solution)/shard_map/while/body/eval_jaxpr/gkij,jgkp->igkp/dot_general | solution.py:56
  105.7 177.0 %all-gather.3.cloned.1.call-done = f32[32,32,128,64]{2,3,1,0:T(8,128)} async-done(((f32[1,32,128,64]{2,3,1,0:T(8,128)}), f32[32,32,128,64]{2,3,1,0:T(8,128)}) %all-gather.3.cloned.1.call-update) | async-done | bytes 33554448 | tf_op jit(solution)/shard_map/all_gather | solution.py:17
  282.7 1.5 broadcast.72
  284.2 178.0 %while.3 = (s32[]{:T(128)}, f32[32,128,64]{2,1,0:T(8,128)}, s32[]{:T(128)}, f32[32,32]{1,0:T(8,128)}, f32[32,32,128,64]{2,3,1,0:T(8,128)}, /*index=5*/s32[]{:T(128)}, s32[]{:T(128)}, s32[]{:T(128)}) while((s32[]{:T(128)}, f32[32,128,64]{2,1,0:T(8,128)}, s32[]{:T(128)}, f32[32,32]{1,0:T(8,128)}, f32[32,32,128,64]{2,3,1,0:T(8,128)}, ...), condition=%wide.region_1.2_spmd, body=%wide.region_0.1_spmd.sunk | while | flops 524293 | bytes 7340551 | solution.py:25
  284.9 1.3 constant_dynamic-slice_fusion.2
  286.8 3.2 bitcast_add_fusion.3
  292.6 3.2 bitcast_add_fusion.3
  298.3 3.2 bitcast_add_fusion.3
  302.2 1.3 constant_dynamic-slice_fusion.2
  304.1 3.2 bitcast_add_fusion.3
  307.9 1.3 constant_dynamic-slice_fusion.2
  309.8 3.2 bitcast_add_fusion.3
  315.6 3.2 bitcast_add_fusion.3
  319.4 1.3 constant_dynamic-slice_fusion.2
  321.3 3.2 bitcast_add_fusion.3
  325.2 1.3 constant_dynamic-slice_fusion.2
  327.1 3.2 bitcast_add_fusion.3
  330.9 1.3 constant_dynamic-slice_fusion.2
  332.8 3.2 bitcast_add_fusion.3
  336.6 1.3 constant_dynamic-slice_fusion.2
  338.5 3.2 bitcast_add_fusion.3
  342.4 1.3 constant_dynamic-slice_fusion.2
  344.3 3.2 bitcast_add_fusion.3
  348.1 1.3 constant_dynamic-slice_fusion.2
  350.0 3.2 bitcast_add_fusion.3
  353.9 1.3 constant_dynamic-slice_fusion.2
  355.8 3.2 bitcast_add_fusion.3
  359.6 1.3 constant_dynamic-slice_fusion.2
  361.5 3.2 bitcast_add_fusion.3
  365.3 1.3 constant_dynamic-slice_fusion.2
  367.2 3.2 bitcast_add_fusion.3
  371.1 1.3 constant_dynamic-slice_fusion.2
  373.0 3.2 bitcast_add_fusion.3
  378.7 3.2 bitcast_add_fusion.3
  384.5 3.2 bitcast_add_fusion.3
  390.2 3.2 bitcast_add_fusion.3
  396.0 3.2 bitcast_add_fusion.3
  401.7 3.2 bitcast_add_fusion.3
  407.5 3.2 bitcast_add_fusion.3
  413.2 3.2 bitcast_add_fusion.3
  418.9 3.2 bitcast_add_fusion.3
  424.7 3.2 bitcast_add_fusion.3
  430.4 3.2 bitcast_add_fusion.3
  436.2 3.2 bitcast_add_fusion.3
  441.9 3.2 bitcast_add_fusion.3
  447.6 3.2 bitcast_add_fusion.3
  453.4 3.2 bitcast_add_fusion.3
  459.1 3.2 bitcast_add_fusion.3
  462.3 1.9 convert_element_type.68
  464.5 3.1 fusion.11
  467.6 1.4 fusion.21
  469.7 18.8 %all_to_all.51 = bf16[4,64,2048]{2,1,0:T(8,128)(2,1)S(1)} all-to-all(bf16[4,64,2048]{2,1,0:T(8,128)(2,1)S(1)} %bitcast.118), channel_id=1, replica_groups=mesh['rollout'=2,'context'=32,'head'=4] {'head'}, dimensions={0} | all-to-all | bytes 2097152 | tf_op jit(solution)/shard_map/all_to_all | solution.py:195
  (159 shorter events, 83.1 us)
Async XLA Ops:
  8.3 9.7 %collective-permute-start = (bf16[4,10240]{1,0:T(4,128)(2,1)S(1)}, bf16[4,10240]{1,0:T(4,128)(2,1)S(1)}, u32[]{:S(2)}, u32[]{:S(2)}) collective-permute-start(bf16[4,10240]{1,0:T(4,128)(2,1)S(1)} %pad_maximum_fusion), channel_id=1, source_target_pairs={{0,1},{1,2},{2,3},{3,4},{4,5},{5,6},{6,7},{7,8},{8,9},{9,10},{10,1... | collective-permute-start | bytes 245768 | tf_op jit(solution)/shard_map/ppermute | solution.py:12
  16.0 2.0 copy-start.12
  18.0 5.4 %copy-start.5 = (bf16[64,8192]{1,0:T(8,128)(2,1)S(1)}, bf16[64,8192]{1,0:T(8,128)(2,1)}, u32[]{:S(2)}) copy-start(bf16[64,8192]{1,0:T(8,128)(2,1)} %param.12) | copy-start | bytes 3145732
  19.2 10.8 %all-to-all-start.1 = ((bf16[64,4,512]{2,0,1:T(8,128)(2,1)}), bf16[64,4,512]{2,0,1:T(8,128)(2,1)S(1)}, u32[]{:S(2)}, u32[]{:S(2)}) async-start(bf16[64,4,512]{2,0,1:T(8,128)(2,1)} %bitcast.111), calls=%async_computation.1 | async-start | bytes 524288 | tf_op jit(solution)/shard_map/all_to_all | solution.py:136
  25.0 8.6 %copy-start.17 = (f32[32]{0:T(128)S(1)}, f32[32]{0:T(128)}, u32[]{:S(2)}) copy-start(f32[32]{0:T(128)} %param.16) | copy-start | bytes 388
  30.0 17.2 %all-to-all-start = ((bf16[64,4,2048]{2,0,1:T(8,128)(2,1)}), bf16[64,4,2048]{2,0,1:T(8,128)(2,1)S(1)}, u32[]{:S(2)}, u32[]{:S(2)}) async-start(bf16[64,4,2048]{2,0,1:T(8,128)(2,1)} %bitcast.110), calls=%async_computation | async-start | bytes 2097152 | tf_op jit(solution)/shard_map/all_to_all | solution.py:135
  33.6 249.1 %all-gather.3.cloned.1.call-start = ((), (), s32[]{:S(2)}) async-start(), calls=%async_computation.3 | async-start | bytes 34603008 | tf_op jit(solution)/shard_map/all_gather | solution.py:17
  53.6 1.2 copy-start.18
  53.6 2.1 copy-start.9
  53.6 2.8 copy-start.8
  53.6 3.5 copy-start.6
  54.7 42.5 %copy-start.7 = (bf16[256,2,1,128]{3,2,1,0:T(2,128)(2,1)S(1)}, bf16[256,2,1,128]{3,2,1,0:T(2,128)(2,1)}, u32[]{:S(2)}) copy-start(bf16[256,2,1,128]{3,2,1,0:T(2,128)(2,1)} %get-tuple-element.147) | copy-start | bytes 393220
  98.5 1.9 copy-start.1
  98.5 1.8 copy-start.11
  98.5 1.8 copy-start.13
  98.6 1.8 copy-start.15
  462.3 1.9 copy-start.2
  462.3 2.2 copy-start.3
  462.3 2.2 copy-start.14
  464.4 3.2 copy-start
  464.4 3.2 copy-start.4
  464.4 3.2 copy-start.10
  464.4 3.2 copy-start.16
Sparse Core Ops, SparseCore 0:
  54.9 227.7 all-gather.2
where the time goes:
time: 500 us; the launch traced here: 496 us
  waiting for transfers between devices  192 us (38%)
  other arithmetic  107 us (21%)
  local copies, waits for them, and re-layouts  103 us (21%)
  blocking collectives  57 us (11%)
  between operations  13.8 us (3%)
  matrix products  12.1 us (2%)
  starting transfers between devices  11.2 us (2%)
    all_gather x1, waiting for transfers between devices, prefix(): gathered = jax.tree.map(lambda a: lax.all_gather(a, axis), part)  177 us
    add x31, other arithmetic, chain_combine(): later[0][:, None, None] * earlier[1] + later[1]  97.7 us
    dynamic_slice x62, local copies, waits for them, and re-layouts, one(): lax.dynamic_index_in_dim(a, lap, 0, False)  58.8 us
    all_gather x1, blocking collectives, prefix(): gathered = jax.tree.map(lambda a: lax.all_gather(a, axis), part)  38.2 us
    mul x31, local copies, waits for them, and re-layouts, chain_combine(): later[0][:, None, None] * earlier[1] + later[1]  21.1 us
    all_to_all x1, blocking collectives, on_device(): lax.all_to_all(head_rows, 'head', split_axis=0, concat_axis=1, tiled=True)  18.8 us
    all_to_all x1, waiting for transfers between devices, on_device(): lax.all_to_all(outgoing_inner, 'head', split_axis=1, concat_axis=0, tiled...  11 us
  transfers between devices with their start and end apart: 4, of which 3 were waited for; matrix products, arithmetic and copies ran while one was open for 5% of the time, Pallas kernels for 0%

commit v1 on v0

--- a/solution.py
+++ b/solution.py
@@ -4,6 +4,22 @@
 from jax.sharding import PartitionSpec as P
 
 BLOCK = 256
+
+
+def pairwise_exchange(shard, axis, split, join):
+    ways, here = (lax.axis_size(axis), lax.axis_index(axis))
+    width = shard.shape[split] // ways
+    dims = list(shard.shape)
+    dims[split] = width
+    height = dims[join]
+    dims[join] = height * ways
+    full = jnp.zeros(dims, shard.dtype)
+    for mask in range(ways):
+        part = lax.dynamic_slice_in_dim(shard, (here ^ mask) * width, width, axis=split)
+        if mask:
+            part = lax.ppermute(part, axis, [(d, d ^ mask) for d in range(ways)])
+        full = lax.dynamic_update_slice_in_dim(full, part, (here ^ mask) * height, axis=join)
+    return full
 
 
 def from_behind(block, axis, distance):
@@ -132,7 +148,7 @@
     outgoing_inner = convolve(inner_raw, before[:, :inner_full], conv_inner)
     outgoing_pairs = convolve(pairs_flat, before[:, inner_full:], conv_flat)
     got_inner, got_pairs = (
-        lax.all_to_all(outgoing_inner, "head", split_axis=1, concat_axis=0, tiled=True),
+        pairwise_exchange(outgoing_inner, "head", 1, 0),
         lax.all_to_all(outgoing_pairs, "head", split_axis=1, concat_axis=0, tiled=True),
     )
     length = got_inner.shape[0]

time: 500 us -> 509 us (1.018)
  other arithmetic: 107 us -> 120 us
  waiting for transfers between devices: 192 us -> 203 us
  local copies, waits for them, and re-layouts: 103 us -> 95.5 us
  matrix products: 12.1 us -> 6.4 us
    mul x31, local copies, waits for them, and re-layouts: 21.1 us -> 0.38 us  [chain_combine(): later[0][:, None, None] * earlier[1] + later[1]]
    dynamic_update_slice x0 -> x4, local copies, waits for them, and re-layouts: none -> 13.9 us  [pairwise_exchange(): lax.dynamic_update_slice_in_dim(full, part, (here ^ mask) * height, axis=...]
    all_to_all x1, waiting for transfers between devices: 3.97 us -> 17.6 us  [on_device(): lax.all_to_all(outgoing_pairs, 'head', split_axis=1, concat_axis=0, tiled...]
    all_to_all x1 -> x0, waiting for transfers between devices: 11 us -> none  [on_device(): lax.all_to_all(outgoing_inner, 'head', split_axis=1, concat_axis=0, tiled...]
    convert_element_type x2, other arithmetic: 1.69 us -> 10.7 us  [convolve(): return jax.nn.silu(summed).astype(jnp.bfloat16)]
    all_gather x1, waiting for transfers between devices: 177 us -> 186 us  [prefix(): gathered = jax.tree.map(lambda a: lax.all_gather(a, axis), part)]
  transfers between devices with their start and end apart: 4 -> 6, of which waited for: 3 -> 2; matrix products, arithmetic and copies ran while one was open for 5% -> 6% of each run, Pallas kernels for 0% -> 0%
where the time goes in v1:
time: 509 us; the launch traced here: 506 us
  waiting for transfers between devices  203 us (40%)
  other arithmetic  120 us (24%)
  local copies, waits for them, and re-layouts  95.5 us (19%)
  blocking collectives  55 us (11%)
  between operations  13.9 us (3%)
  starting transfers between devices  11.6 us (2%)
  matrix products  6.4 us (1%)
    all_gather x1, waiting for transfers between devices, prefix(): gathered = jax.tree.map(lambda a: lax.all_gather(a, axis), part)  186 us
    add x31, other arithmetic, chain_combine(): later[0][:, None, None] * earlier[1] + later[1]  99.1 us
    dynamic_slice x62, local copies, waits for them, and re-layouts, one(): lax.dynamic_index_in_dim(a, lap, 0, False)  58.8 us
    all_gather x1, blocking collectives, prefix(): gathered = jax.tree.map(lambda a: lax.all_gather(a, axis), part)  36.2 us
    all_to_all x1, blocking collectives, on_device(): lax.all_to_all(head_rows, 'head', split_axis=0, concat_axis=1, tiled=True)  18.8 us
    all_to_all x1, waiting for transfers between devices, on_device(): lax.all_to_all(outgoing_pairs, 'head', split_axis=1, concat_axis=0, tiled...  17.6 us
    dynamic_update_slice x4, local copies, waits for them, and re-layouts, pairwise_exchange(): lax.dynamic_update_slice_in_dim(full, part, (here ^ mask) * height, axis=...  13.9 us
    convert_element_type x2, other arithmetic, convolve(): return jax.nn.silu(summed).astype(jnp.bfloat16)  10.7 us
  transfers between devices with their start and end apart: 6, of which 2 were waited for; matrix products, arithmetic and copies ran while one was open for 6% of the time, Pallas kernels for 0%

profile of v1, /device:TPU:230, one launch (start us, length us, event | category | flops | bytes accessed | tf_op | source)
XLA Modules:
  0.0 506.1 jit_solution(387901333851609167)
XLA Ops:
  9.0 3.5 collective-permute-start
  12.5 2.6 fusion.45
  19.1 1.4 fusion.46
  23.6 1.8 copy.78
  25.5 2.6 maximum_convert_fusion
  28.2 10.4 %multiply_convert_fusion.2 = bf16[64,8192]{0,1:T(8,128)(2,1)S(1)} fusion(f32[68,8192]{0,1:T(8,128)S(1)} %maximum_convert_fusion, f32[8192]{0:T(1024)S(1)} %bitcast.111, f32[8192]{0:T(1024)S(1)} %bitcast.112, f32[8192]{0:T(1024)S(1)} %bitcast.109, f32[8192]{0:T(1024)S(1)} %bitcast.110, f32[8192]{0:T(1024)S(1)} %bitcast.108), kind=kLoop, calls=%fused_computation.18 | loop fusion | flops 6815744 | bytes 9601024 | tf_op jit(solution)/shard_map/convert_element_type | solution.py:51
  39.8 1.6 collective-permute-start.1
  41.3 1.3 collective-permute-start.2
  42.7 1.8 collective-permute-start.3
  46.4 3.4 all-to-all-start
  51.3 2.4 dynamic_update_slice.32
  53.7 17.6 %all-to-all-done = bf16[64,4,512]{2,0,1:T(8,128)(2,1)S(1)} async-done(((bf16[64,4,512]{2,0,1:T(8,128)(2,1)}), bf16[64,4,512]{2,0,1:T(8,128)(2,1)S(1)}, u32[]{:S(2)}, u32[]{:S(2)}) %all-to-all-start) | async-done | bytes 262176 | tf_op jit(solution)/shard_map/all_to_all | solution.py:152
  71.7 5.9 %dynamic_update_slice.33 = bf16[256,2048]{0,1:T(8,128)(2,1)S(1)} dynamic-update-slice(bf16[256,2048]{0,1:T(8,128)(2,1)S(1)} %dynamic_update_slice.32, bf16[64,2048]{0,1:T(8,128)(2,1)} %collective-permute-done.1, s32[]{:T(128)S(6)} %select_n.44, s32[]{:T(128)} %constant.105.clone.1) | dynamic-update-slice | bytes 524292 | tf_op jit(solution)/shard_map/dynamic_update_slice | solution.py:21
  77.7 2.0 dynamic_update_slice.34
  79.7 3.6 dynamic_update_slice.35
  85.4 1.3 copy.90
  86.8 36.2 %all-gather = f32[32,1,32]{2,1,0:T(1,128)S(1)} all-gather(f32[1,1,32]{2,1,0:T(1,128)S(1)} %copy-done.20), channel_id=2, replica_groups=mesh['rollout'=2,'context'=32,'head'=4] {'context'}, dimensions={0}, use_global_device_ids=true | all-gather | bytes 4224 | tf_op jit(solution)/shard_map/all_gather | solution.py:33
  123.3 4.2 fusion
  127.5 185.5 %all-gather.3.cloned.1.call-done = f32[32,32,128,64]{2,3,1,0:T(8,128)} async-done(((f32[1,32,128,64]{2,3,1,0:T(8,128)}), f32[32,32,128,64]{2,3,1,0:T(8,128)}) %all-gather.3.cloned.1.call-update) | async-done | bytes 33554448 | tf_op jit(solution)/shard_map/all_gather | solution.py:33
  313.0 1.6 broadcast.61
  314.6 158.9 %while.3 = (s32[]{:T(128)}, f32[32,128,64]{2,1,0:T(8,128)}, s32[]{:T(128)}, f32[32,32]{1,0:T(8,128)S(1)}, f32[32,32,128,64]{2,3,1,0:T(8,128)}, /*index=5*/s32[]{:T(128)}, s32[]{:T(128)}, s32[]{:T(128)}) while((s32[]{:T(128)}, f32[32,128,64]{2,1,0:T(8,128)}, s32[]{:T(128)}, f32[32,32]{1,0:T(8,128)S(1)}, f32[32,32,128,64]{2,3,1,0:T(8,128)}, ...), condition=%wide.region_1.2_spmd, body=%wide.region_0.1_spmd.sunk | while | flops 524293 | bytes 7340543 | solution.py:41
  316.5 3.2 bitcast_add_fusion.3
  319.7 1.3 constant_dynamic-slice_fusion.6
  321.6 3.2 bitcast_add_fusion.3
  326.8 3.2 bitcast_add_fusion.3
  329.9 1.3 constant_dynamic-slice_fusion.6
  331.9 3.2 bitcast_add_fusion.3
  337.0 3.2 bitcast_add_fusion.3
  340.2 1.3 constant_dynamic-slice_fusion.6
  342.1 3.2 bitcast_add_fusion.3
  347.3 3.2 bitcast_add_fusion.3
  350.4 1.3 constant_dynamic-slice_fusion.6
  352.4 3.2 bitcast_add_fusion.3
  355.6 1.3 constant_dynamic-slice_fusion.6
  357.5 3.2 bitcast_add_fusion.3
  360.7 1.3 constant_dynamic-slice_fusion.6
  362.6 3.2 bitcast_add_fusion.3
  365.8 1.3 constant_dynamic-slice_fusion.6
  367.8 3.2 bitcast_add_fusion.3
  372.9 3.2 bitcast_add_fusion.3
  376.1 1.3 constant_dynamic-slice_fusion.6
  378.0 3.2 bitcast_add_fusion.3
  383.1 3.2 bitcast_add_fusion.3
  386.3 1.3 constant_dynamic-slice_fusion.6
  388.3 3.2 bitcast_add_fusion.3
  393.4 3.2 bitcast_add_fusion.3
  398.5 3.2 bitcast_add_fusion.3
  403.6 3.2 bitcast_add_fusion.3
  408.8 3.2 bitcast_add_fusion.3
  413.9 3.2 bitcast_add_fusion.3
  419.0 3.2 bitcast_add_fusion.3
  424.1 3.2 bitcast_add_fusion.3
  429.3 3.2 bitcast_add_fusion.3
  434.4 3.2 bitcast_add_fusion.3
  439.5 3.2 bitcast_add_fusion.3
  444.6 3.2 bitcast_add_fusion.3
  449.8 3.2 bitcast_add_fusion.3
  454.9 3.2 bitcast_add_fusion.3
  460.0 3.2 bitcast_add_fusion.3
  465.1 3.2 bitcast_add_fusion.3
  470.3 3.2 bitcast_add_fusion.3
  473.5 1.9 convert_element_type.54
  477.0 1.4 bitcast_reduce_fusion
  479.4 18.8 %all_to_all.35 = bf16[4,64,2048]{2,1,0:T(8,128)(2,1)S(1)} all-to-all(bf16[4,64,2048]{2,1,0:T(8,128)(2,1)S(1)} %bitcast.102), channel_id=1, replica_groups=mesh['rollout'=2,'context'=32,'head'=4] {'head'}, dimensions={0} | all-to-all | bytes 2097152 | tf_op jit(solution)/shard_map/all_to_all | solution.py:211
  (168 shorter events, 68.2 us)
Async XLA Ops:
  6.5 13.9 %copy-start.4 = (bf16[64,8192]{1,0:T(8,128)(2,1)S(1)}, bf16[64,8192]{1,0:T(8,128)(2,1)}, u32[]{:S(2)}) copy-start(bf16[64,8192]{1,0:T(8,128)(2,1)} %param.12) | copy-start | bytes 3145732
  9.0 13.7 %collective-permute-start = (bf16[4,10240]{1,0:T(4,128)(2,1)}, bf16[4,10240]{1,0:T(4,128)(2,1)}, u32[]{:S(2)}, u32[]{:S(2)}) collective-permute-start(bf16[4,10240]{1,0:T(4,128)(2,1)} %pad_maximum_fusion), channel_id=1, source_target_pairs={{0,1},{1,2},{2,3},{3,4},{4,5},{5,6},{6,7},{7,8},{8,9},{9,10},{10,1... | collective-permute-start | bytes 245768 | tf_op jit(solution)/shard_map/ppermute | solution.py:28
  17.6 2.9 copy-start.16
  17.7 2.8 copy-start.6
  25.4 2.7 copy-start.7
  25.4 2.7 copy-start.8
  25.5 2.7 copy-start.9
  25.5 2.7 copy-start.10
  25.5 2.7 copy-start.11
  38.5 6.7 %copy-start.13 = (f32[1,8,2,128]{3,2,1,0:T(2,128)S(1)}, f32[1,8,2,128]{3,2,1,0:T(2,128)}, u32[]{:S(2)}) copy-start(f32[1,8,2,128]{3,2,1,0:T(2,128)} %get-tuple-element.167) | copy-start | bytes 24580
  38.5 6.7 %copy-start.14 = (f32[1,8,2,128]{3,2,1,0:T(2,128)S(1)}, f32[1,8,2,128]{3,2,1,0:T(2,128)}, u32[]{:S(2)}) copy-start(f32[1,8,2,128]{3,2,1,0:T(2,128)} %get-tuple-element.168) | copy-start | bytes 24580
  38.6 6.7 %copy-start.15 = (f32[1,8,2,128]{3,2,1,0:T(2,128)S(1)}, f32[1,8,2,128]{3,2,1,0:T(2,128)}, u32[]{:S(2)}) copy-start(f32[1,8,2,128]{3,2,1,0:T(2,128)} %get-tuple-element.169) | copy-start | bytes 24580
  39.8 31.9 %collective-permute-start.1 = (bf16[64,2048]{0,1:T(8,128)(2,1)}, bf16[64,2048]{0,1:T(8,128)(2,1)}, u32[]{:S(2)}, u32[]{:S(2)}) collective-permute-start(bf16[64,2048]{0,1:T(8,128)(2,1)} %get-tuple-element.151), channel_id=1, source_target_pairs={{0,1},{1,0},{2,3},{3,2},{4,5},{5,4},{6,7},{7,6},{8,9},{9,8},{10,11... | collective-permute-start | bytes 786440 | tf_op jit(solution)/shard_map/ppermute | solution.py:20
  41.3 36.3 %collective-permute-start.2 = (bf16[64,2048]{0,1:T(8,128)(2,1)}, bf16[64,2048]{0,1:T(8,128)(2,1)S(1)}, u32[]{:S(2)}, u32[]{:S(2)}) collective-permute-start(bf16[64,2048]{0,1:T(8,128)(2,1)} %get-tuple-element.150), channel_id=1, source_target_pairs={{0,2},{1,3},{2,0},{3,1},{4,6},{5,7},{6,4},{7,5},{8,10},{9,11},{10,... | collective-permute-start | bytes 786440 | tf_op jit(solution)/shard_map/ppermute | solution.py:20
  42.7 37.0 %collective-permute-start.3 = (bf16[64,2048]{0,1:T(8,128)(2,1)}, bf16[64,2048]{0,1:T(8,128)(2,1)S(1)}, u32[]{:S(2)}, u32[]{:S(2)}) collective-permute-start(bf16[64,2048]{0,1:T(8,128)(2,1)} %get-tuple-element.149), channel_id=1, source_target_pairs={{0,3},{1,2},{2,1},{3,0},{4,7},{5,6},{6,5},{7,4},{8,11},{9,10},{10,... | collective-permute-start | bytes 786440 | tf_op jit(solution)/shard_map/ppermute | solution.py:20
  46.4 24.8 %all-to-all-start = ((bf16[64,4,512]{2,0,1:T(8,128)(2,1)}), bf16[64,4,512]{2,0,1:T(8,128)(2,1)S(1)}, u32[]{:S(2)}, u32[]{:S(2)}) async-start(bf16[64,4,512]{2,0,1:T(8,128)(2,1)} %bitcast.94), calls=%async_computation | async-start | bytes 524288 | tf_op jit(solution)/shard_map/all_to_all | solution.py:152
  49.8 263.2 %all-gather.3.cloned.1.call-start = ((), (), s32[]{:S(2)}) async-start(), calls=%async_computation.2 | async-start | bytes 34603008 | tf_op jit(solution)/shard_map/all_gather | solution.py:33
  71.3 12.0 %copy-start.12 = (f32[256,32]{0,1:T(8,128)S(1)}, f32[256,32]{0,1:T(8,128)}, u32[]{:S(2)}) copy-start(f32[256,32]{0,1:T(8,128)} %copy.86) | copy-start | bytes 98308
  83.3 40.0 %copy-start = (bf16[256,2048]{0,1:T(8,128)(2,1)}, bf16[256,2048]{0,1:T(8,128)(2,1)S(1)}, u32[]{:S(2)}) copy-start(bf16[256,2048]{0,1:T(8,128)(2,1)S(1)} %dynamic_update_slice.35) | copy-start | bytes 3145732
  83.8 1.6 copy-start.5
  84.9 1.8 copy-start.19
  84.9 1.9 copy-start.20
  84.9 38.4 %copy-start.17 = (f32[32,256]{1,0:T(8,128)S(1)}, f32[32,256]{1,0:T(8,128)}, u32[]{:S(2)}) copy-start(f32[32,256]{1,0:T(8,128)} %copy-done.16) | copy-start | bytes 98308
  473.5 2.5 copy-start.3
  475.4 1.3 copy-start.1
  475.4 1.6 copy-start.2
  477.0 1.4 copy-start.18
Sparse Core Ops, SparseCore 0:
  85.0 227.9 all-gather.2
